TPU v7x, 128 devices: a whole 4x4x4 slice. The times are simulated.
128 devices in a mesh: pix: 8 (over z, y_lo), mem: 16 (over y_hi, x, core).
Axes of the slice: x: 4, y: 4 (y_hi: 2, y_lo: 2; y = y_hi * 2 + y_lo), z: 4, core: 2. Of those that a mesh axis runs over, the one named last changes fastest.
Arguments:
- alpha: bfloat16 [16, 1024, 32, 128], P('mem', 'pix'), may hold values from -6 to 6
- perturbations: bfloat16 [16, 1024, 32, 128], P('mem', 'pix'), may hold values from -6 to 6
- loc_weights: bfloat16 [1024, 9, 128, 128], P('pix'), may hold values from -0.1875 to 0.1875
- static_ctl: float32 [1024, 32, 128], P('pix'), may hold values from -6 to 6
- static_sd: bfloat16 [1024, 32, 128], P('pix'), may hold values from 0.5 to 2
- innovation: float32 [1024, 32, 128], P('pix'), may hold values from -6 to 6
- obs_weight: bfloat16 [1024, 32, 128], P('pix'), may hold values from 0.25 to 4
- neighbours: int32 [1024, 9], P('pix'), may hold values from 0 to 255, as said below
- outbound_blocks: int32 [8, 8, 16], replicated, may hold values from 0 to 127, as said below
- send_counts: int32 [8, 8], replicated, may hold values from 0 to 16, as said below
Outputs:
- increment: float32 [1024, 32, 128], P('pix')
- grad_static: float32 [1024, 32, 128], P('pix')
- grad_alpha: float32 [16, 1024, 32, 128], P('mem', 'pix')
Inputs may be any that keep to these rules, and one draw needn't show every extreme that they name: neighbours[b, s] for s = 0 is b % 128. An entry below 128 names a block of the same shard; an entry n of 128 or more names halo slot n - 128 = p * 16 + c of that shard, the c-th block that shard p sends to it, and then c < send_counts[p, shard] and p is the shard just below or just above it. outbound_blocks[p, q] holds 16 distinct block numbers local to shard p; the first send_counts[p, q] of them are sent to shard q. send_counts[p, q] is 0 unless q = p - 1 or q = p + 1 (no wrap); those entries lie between 8 and 16, and send_counts[0, 1] equals 16.
All inputs are finite; a program needn't handle non-finite values.
Results may differ from a plain program's by a relative error of at most 0.0022.
Values may be sent and summed in bfloat16 or wider, within the bound.
A program may use at most 192 MiB of HBM per device.

v0:
```python
import functools
import math

import jax
import jax.numpy as jnp
from jax import lax
from jax.experimental import pallas as pl
from jax.experimental.pallas import tpu as pltpu
from jax.sharding import PartitionSpec as P

F32, BF16 = jnp.float32, jnp.bfloat16
MESH = pl.DeviceIdType.MESH
HBM = pl.BlockSpec(memory_space=pl.ANY)
VMEM = pl.BlockSpec(memory_space=pltpu.VMEM)
SMEM = pl.BlockSpec(memory_space=pltpu.SMEM)
LIMIT = 62 * 2**20


def remote(src, dst, send, recv, device):
    return pltpu.make_async_remote_copy(
        src_ref=src, dst_ref=dst, send_sem=send, recv_sem=recv, device_id=device, device_id_type=MESH
    )


def meet(devices):
    barrier = pltpu.get_barrier_semaphore()
    for device in devices:
        pl.semaphore_signal(barrier, inc=1, device_id=device, device_id_type=MESH)
    pl.semaphore_wait(barrier, len(devices))


def places(shards, members):
    pix, mem = lax.axis_index("pix"), lax.axis_index("mem")
    core = lax.rem(mem, 2)
    partner = (pix, mem + 1 - 2 * core)
    below = (lax.rem(pix + shards - 1, shards), mem)
    above = (lax.rem(pix + 1, shards), mem)
    return pix, mem, core, partner, below, above


def forward_kernel(
    dims, table, alpha_h, pert_h, w_h, ens_h, other_pert_h,
    alpha_v, mine, theirs, pert0, pert1, wv, terms, recv, gathered, other, packed,
    w_sem, local_sem, out_sem, pair_send, pair_recv, halo_send, halo_recv, rs_send, rs_recv, ag_send, ag_recv,
):
    shards, members, blocks, neigh, cap = dims
    half, chips = blocks // 2, members // 2
    per = half // chips
    pix, mem, core, partner, below, above = places(shards, members)
    chip = mem // 2

    def w_copy(step):
        k = lax.rem(chip + 1 + step, chips)
        return pltpu.make_async_copy(
            w_h.at[pl.ds(core * half + k * per, per)], wv.at[pl.ds(k * per, per)], w_sem.at[step]
        )

    loads = [
        pltpu.make_async_copy(alpha_h, alpha_v, local_sem.at[0]),
        pltpu.make_async_copy(alpha_h, mine.at[pl.ds(0, blocks)], local_sem.at[1]),
        pltpu.make_async_copy(pert_h.at[pl.ds(core * half, half)], pert0, local_sem.at[2]),
    ]
    for load in loads:
        load.start()
    for step in range(chips):
        w_copy(step).start()
    zero = jnp.zeros(mine.shape[1:], BF16)
    mine[blocks + 2 * cap] = zero
    theirs[blocks + 2 * cap] = zero
    peers = [(pix, 2 * lax.rem(chip + j, chips) + core) for j in range(1, chips)]
    meet([partner, below, above] + peers)
    pair = [
        remote(alpha_h, theirs.at[pl.ds(0, blocks)], pair_send.at[0], pair_recv.at[0], partner),
        remote(pert_h.at[pl.ds((1 - core) * half, half)], pert1, pair_send.at[1], pair_recv.at[1], partner),
        remote(
            mine.at[pl.ds(blocks, 2 * cap)], theirs.at[pl.ds(blocks, 2 * cap)], pair_send.at[2], pair_recv.at[2], partner
        ),
    ]
    loads[0].wait()
    base = half * neigh
    for c in range(2 * cap):
        keep = table[base + 2 * cap + c].astype(F32)
        packed[c] = (alpha_v[table[base + c]].astype(F32) * keep).astype(BF16)
    halo = [
        remote(packed.at[pl.ds(0, cap)], mine.at[pl.ds(blocks + cap, cap)], halo_send.at[0], halo_recv.at[1], below),
        remote(packed.at[pl.ds(cap, cap)], mine.at[pl.ds(blocks, cap)], halo_send.at[1], halo_recv.at[0], above),
    ]
    halo[0].start()
    halo[1].start()
    pair[0].start()
    pair[1].start()
    halo[0].wait_recv()
    halo[1].wait_recv()
    pair[2].start()
    loads[1].wait()
    loads[2].wait()
    for copy in pair:
        copy.wait_recv()

    def rs_copy(k):
        return remote(
            terms.at[pl.ds(k * per, per)], recv.at[chip], rs_send.at[k], rs_recv.at[chip], (pix, 2 * k + core)
        )

    def one_step(step, carry):
        k = lax.rem(chip + 1 + step, chips)
        w_copy(step).wait()
        for j in range(per):
            i = k * per + j
            picked = [table[i * neigh + s] for s in range(neigh)]
            rows = jnp.concatenate(
                [jnp.concatenate([field[n] for n in picked], axis=1) for field in (mine, theirs)], axis=0
            )
            weights = wv[i].reshape(neigh * wv.shape[2], wv.shape[3])
            local = jnp.dot(rows, weights, preferred_element_type=F32)
            ch = local.shape[0] // 2
            terms[i] = pert0[i].astype(F32) * local[:ch] + pert1[i].astype(F32) * local[ch:]

        @pl.when(step < chips - 1)
        def _():
            rs_copy(k).start()

        return carry

    lax.fori_loop(0, chips, one_step, 0)
    other_pert = pltpu.make_async_copy(pert1, other_pert_h, out_sem.at[2])
    other_pert.start()
    for j in range(1, chips):
        src = lax.rem(chip + j, chips)
        remote(terms.at[pl.ds(0, per)], recv.at[src], rs_send.at[src], rs_recv.at[src], partner).wait_recv()
    recv[chip] = terms[pl.ds(chip * per, per)]
    spread = 1.0 / math.sqrt(members - 1)
    for i in range(per):
        total = recv[0, i]
        for k in range(1, chips):
            total = total + recv[k, i]
        gathered[chip, i] = total * spread
    sends = [
        remote(gathered.at[chip], gathered.at[chip], ag_send.at[j - 1], ag_recv.at[chip], peers[j - 1])
        for j in range(1, chips)
    ]
    for copy in sends:
        copy.start()
    for j in range(1, chips):
        src = lax.rem(chip + j, chips)
        remote(gathered.at[src], gathered.at[src], ag_send.at[j - 1], ag_recv.at[src], partner).wait_recv()
    swap = remote(gathered, other, pair_send.at[3], pair_recv.at[3], partner)
    swap.start()
    outs = [
        pltpu.make_async_copy(gathered, ens_h.at[pl.ds(core * chips, chips)], out_sem.at[0]),
        pltpu.make_async_copy(other, ens_h.at[pl.ds((1 - core) * chips, chips)], out_sem.at[1]),
    ]
    outs[0].start()
    swap.wait_recv()
    outs[1].start()
    for copy in halo + pair + [swap] + sends:
        copy.wait_send()
    for j in range(1, chips):
        rs_copy(lax.rem(chip + j, chips)).wait_send()
    for copy in outs + [other_pert]:
        copy.wait()


def adjoint_kernel(
    dims, table, where, ens_h, ctl_h, dev_h, inn_h, wgt_h, pert_h, other_pert_h, w_h, inc_h, gs_h, acc_out, send_out,
    ens, ctl, dev, inn, wgt, pert0, pert1, wv, inc, gs, acc0, acc1, w_sem, in_sem, out_sem,
):
    shards, members, blocks, neigh, cap = dims
    half = blocks // 2
    chunks = w_sem.shape[0]
    per = half // chunks
    core = where[0]
    spread = 1.0 / math.sqrt(members - 1)
    starts = (core * half, (1 - core) * half)
    loads = [
        [
            pltpu.make_async_copy(src.at[pl.ds(starts[h], half)], dst.at[h], in_sem.at[h, n])
            for n, (src, dst) in enumerate(
                ((ens_h, ens), (ctl_h, ctl), (dev_h, dev), (inn_h, inn), (wgt_h, wgt))
            )
        ]
        for h in range(2)
    ]
    loads[0] += [
        pltpu.make_async_copy(pert_h.at[pl.ds(core * half, half)], pert0, in_sem.at[0, 5]),
        pltpu.make_async_copy(other_pert_h, pert1, in_sem.at[0, 6]),
    ]

    def w_copy(j):
        return pltpu.make_async_copy(
            w_h.at[pl.ds(core * half + j * per, per)], wv.at[pl.ds(j * per, per)], w_sem.at[j]
        )

    for load in loads[0]:
        load.start()
    for j in range(chunks):
        w_copy(j).start()
    for load in loads[1]:
        load.start()
    acc0[...] = jnp.zeros_like(acc0)
    acc1[...] = jnp.zeros_like(acc1)

    def fields(h, i):
        scale = dev[h, i].astype(F32)
        increment = scale * ctl[h, i] + ens[h, i].astype(F32)
        residual = wgt[h, i].astype(F32) * (increment - inn[h, i])
        inc[h, i] = increment
        gs[h, i] = ctl[h, i] + scale * residual
        return residual

    for load in loads[0]:
        load.wait()

    def one_chunk(j, carry):
        w_copy(j).wait()
        for jj in range(per):
            i = j * per + jj
            residual = fields(0, i)
            focus = jnp.concatenate(
                [(p[i].astype(F32) * residual * spread).astype(BF16) for p in (pert0, pert1)], axis=0
            )
            weights = wv[i].reshape(neigh * wv.shape[2], wv.shape[3])
            pieces = lax.dot_general(
                focus, weights, (((1,), (1,)), ((), ())), preferred_element_type=F32
            )
            ch, width = focus.shape[0] // 2, wv.shape[2]
            for s in range(neigh):
                n = table[i * neigh + s]
                acc0[n] += pieces[:ch, s * width : (s + 1) * width]
                acc1[n] += pieces[ch:, s * width : (s + 1) * width]
        return carry

    lax.fori_loop(0, chunks, one_chunk, 0)
    for load in loads[1]:
        load.wait()
    stores = [
        [
            pltpu.make_async_copy(src.at[h], dst.at[pl.ds(starts[h], half)], out_sem.at[h, n])
            for n, (src, dst) in enumerate(((inc, inc_h), (gs, gs_h)))
        ]
        for h in range(2)
    ]
    for store in stores[0]:
        store.start()

    def other_half(i, carry):
        fields(1, i)
        return carry

    lax.fori_loop(0, half, other_half, 0, unroll=4)
    for store in stores[1]:
        store.start()
    last = pltpu.make_async_copy(acc0, acc_out, out_sem.at[0, 2])
    last.start()
    send_out[...] = acc1[pl.ds(0, blocks + 2 * cap)].astype(send_out.dtype)
    last.wait()
    for h in range(2):
        for store in stores[h]:
            store.wait()


def return_kernel(
    dims, acc_h, send_ref, partner_ref, back_ref, half_buf, back_buf, own_rim, rim, packed,
    in_sem, pair_send, pair_recv, halo_send, halo_recv,
):
    shards, members, blocks, neigh, cap = dims
    pix, mem, core, partner, below, above = places(shards, members)
    load = pltpu.make_async_copy(acc_h.at[pl.ds(blocks, 2 * cap)], own_rim, in_sem)
    load.start()
    meet([partner, below, above])
    pair = [
        remote(send_ref.at[pl.ds(blocks, 2 * cap)], rim, pair_send.at[0], pair_recv.at[0], partner),
        remote(send_ref.at[pl.ds(0, blocks)], half_buf, pair_send.at[1], pair_recv.at[1], partner),
    ]
    pair[0].start()
    pair[1].start()
    load.wait()
    pair[0].wait_recv()
    packed[...] = (own_rim[...] + rim[...].astype(F32)).astype(BF16)
    halo = [
        remote(packed.at[pl.ds(0, cap)], back_buf.at[pl.ds(cap, cap)], halo_send.at[0], halo_recv.at[1], below),
        remote(packed.at[pl.ds(cap, cap)], back_buf.at[pl.ds(0, cap)], halo_send.at[1], halo_recv.at[0], above),
    ]
    halo[0].start()
    halo[1].start()
    pair[1].wait_recv()
    partner_ref[...] = half_buf[...]
    halo[0].wait_recv()
    halo[1].wait_recv()
    back_ref[...] = back_buf[...]
    for copy in pair + halo:
        copy.wait_send()


def finish_kernel(dims, table, alpha_ref, acc_ref, partner_ref, back_ref, out_ref):
    shards, members, blocks, neigh, cap = dims
    base = (blocks // 2) * neigh

    def one(i, carry):
        out_ref[i] = alpha_ref[i].astype(F32) + acc_ref[i] + partner_ref[i].astype(F32)
        return carry

    lax.fori_loop(0, blocks, one, 0, unroll=8)
    for c in range(2 * cap):
        out_ref[table[base + c]] += back_ref[c].astype(F32) * table[base + 2 * cap + c].astype(F32)


def per_device(
    alpha, perturbations, loc_weights, static_ctl, static_sd, innovation, obs_weight, neighbours, outbound_blocks,
    send_counts,
):
    shards, members = lax.axis_size("pix"), lax.axis_size("mem")
    me = lax.axis_index("pix")
    core = lax.axis_index("mem") % 2
    alpha, pert = alpha[0], perturbations[0]
    blocks, ch, width = alpha.shape
    neigh, cap = neighbours.shape[1], outbound_blocks.shape[2]
    half, chips = blocks // 2, members // 2
    per, ext = half // chips, blocks + 2 * cap + 1
    dims = (shards, members, blocks, neigh, cap)

    mine = lax.dynamic_slice_in_dim(neighbours, core * half, half, 0)
    slot = mine - blocks
    source = slot // cap
    rim_slot = jnp.where(
        source == me - 1, slot - (me - 1) * cap, jnp.where(source == me + 1, slot - me * cap, 2 * cap)
    )
    targets = jnp.where(mine < blocks, mine, blocks + rim_slot).reshape(half * neigh)
    below, above = (me + shards - 1) % shards, (me + 1) % shards
    rows = jnp.concatenate([outbound_blocks[me, below], outbound_blocks[me, above]])
    rank = jnp.arange(cap, dtype=jnp.int32)
    keep = jnp.concatenate([rank < send_counts[me, below], rank < send_counts[me, above]]).astype(jnp.int32)
    table = jnp.concatenate([targets, rows, keep]).astype(jnp.int32)

    tile = (ch, width)
    dma = pltpu.SemaphoreType.DMA
    ens, other_pert = pl.pallas_call(
        functools.partial(forward_kernel, dims),
        out_shape=(
            jax.ShapeDtypeStruct((members, per, *tile), F32),
            jax.ShapeDtypeStruct((half, *tile), BF16),
        ),
        in_specs=[SMEM, HBM, HBM, HBM],
        out_specs=(HBM, HBM),
        scratch_shapes=[
            pltpu.VMEM((blocks, *tile), BF16),
            pltpu.VMEM((ext, *tile), BF16),
            pltpu.VMEM((ext, *tile), BF16),
            pltpu.VMEM((half, *tile), BF16),
            pltpu.VMEM((half, *tile), BF16),
            pltpu.VMEM((half, neigh, width, width), BF16),
            pltpu.VMEM((half, *tile), F32),
            pltpu.VMEM((chips, per, *tile), F32),
            pltpu.VMEM((chips, per, *tile), F32),
            pltpu.VMEM((chips, per, *tile), F32),
            pltpu.VMEM((2 * cap, *tile), BF16),
            dma((chips,)), dma((3,)), dma((3,)), dma((4,)), dma((4,)), dma((2,)), dma((2,)),
            dma((chips,)), dma((chips,)), dma((chips,)), dma((chips,)),
        ],
        compiler_params=pltpu.CompilerParams(collective_id=0, has_side_effects=True, vmem_limit_bytes=LIMIT),
        name="forward",
    )(table, alpha, pert, loc_weights)

    chunks = max(half // 8, 1)
    increment, grad_static, acc, sending = pl.pallas_call(
        functools.partial(adjoint_kernel, dims),
        out_shape=(
            jax.ShapeDtypeStruct((blocks, *tile), F32),
            jax.ShapeDtypeStruct((blocks, *tile), F32),
            jax.ShapeDtypeStruct((ext, *tile), F32),
            jax.ShapeDtypeStruct((ext - 1, *tile), BF16),
        ),
        in_specs=[SMEM, SMEM] + [HBM] * 8,
        out_specs=(HBM, HBM, HBM, VMEM),
        scratch_shapes=[
            pltpu.VMEM((2, half, *tile), F32),
            pltpu.VMEM((2, half, *tile), F32),
            pltpu.VMEM((2, half, *tile), BF16),
            pltpu.VMEM((2, half, *tile), F32),
            pltpu.VMEM((2, half, *tile), BF16),
            pltpu.VMEM((half, *tile), BF16),
            pltpu.VMEM((half, *tile), BF16),
            pltpu.VMEM((half, neigh, width, width), BF16),
            pltpu.VMEM((2, half, *tile), F32),
            pltpu.VMEM((2, half, *tile), F32),
            pltpu.VMEM((ext, *tile), F32),
            pltpu.VMEM((ext, *tile), F32),
            dma((chunks,)), dma((2, 7)), dma((2, 3)),
        ],
        compiler_params=pltpu.CompilerParams(vmem_limit_bytes=LIMIT),
        name="adjoint",
    )(
        table, core.reshape(1), ens.reshape(blocks, *tile), static_ctl, static_sd, innovation, obs_weight, pert,
        other_pert, loc_weights,
    )

    from_partner, came_back = pl.pallas_call(
        functools.partial(return_kernel, dims),
        out_shape=(
            jax.ShapeDtypeStruct((blocks, *tile), BF16),
            jax.ShapeDtypeStruct((2 * cap, *tile), BF16),
        ),
        in_specs=[HBM, VMEM],
        out_specs=(VMEM, VMEM),
        scratch_shapes=[
            pltpu.VMEM((blocks, *tile), BF16),
            pltpu.VMEM((2 * cap, *tile), BF16),
            pltpu.VMEM((2 * cap, *tile), F32),
            pltpu.VMEM((2 * cap, *tile), BF16),
            pltpu.VMEM((2 * cap, *tile), BF16),
            dma, dma((2,)), dma((2,)), dma((2,)), dma((2,)),
        ],
        compiler_params=pltpu.CompilerParams(collective_id=1, has_side_effects=True, vmem_limit_bytes=LIMIT),
        name="returns",
    )(acc, sending)

    grad_alpha = pl.pallas_call(
        functools.partial(finish_kernel, dims),
        out_shape=jax.ShapeDtypeStruct((blocks, *tile), F32),
        in_specs=[SMEM, VMEM, VMEM, VMEM, VMEM],
        out_specs=VMEM,
        compiler_params=pltpu.CompilerParams(vmem_limit_bytes=LIMIT),
        name="finish",
    )(table, alpha, acc, from_partner, came_back)
    return increment, grad_static, grad_alpha[None]


def solution(mesh):
    placed = (
        P("mem", "pix", None, None),
        P("mem", "pix", None, None),
        P("pix", None, None, None),
        P("pix", None, None),
        P("pix", None, None),
        P("pix", None, None),
        P("pix", None, None),
        P("pix", None),
        P(),
        P(),
    )
    return jax.shard_map(
        per_device,
        mesh=mesh,
        in_specs=placed,
        out_specs=(P("pix", None, None), P("pix", None, None), P("mem", "pix", None, None)),
        check_vma=False,
    )
```

profile of v0, /device:TPU:1, one launch (start us, length us, event | category | flops | bytes accessed | tf_op | source)
XLA Modules:
  0.0 96.6 jit_solution(7934810222625127431)
XLA Ops:
  0.7 0.8 fusion.3
  1.5 1.3 %fusion.5 = (s32[1,1]{1,0:T(1,128)}, s32[1,1]{1,0:T(1,128)}) fusion(s32[8,8]{1,0:T(8,128)} %param.19, s32[]{:T(128)S(6)} %select_n.53, s32[]{:T(128)S(6)} %select_n.55, s32[]{:T(128)S(6)} %select_n.57), kind=kLoop, calls=%fused_computation.18 | loop fusion | bytes 28 | tf_op jit(solution)/shard_map/dynamic_slice | solution.py:332
  2.8 1.3 %iota_compare_fusion = (pred[16]{0:T(512)(128)(4,1)S(1)}, pred[16]{0:T(512)(128)(4,1)S(1)}) fusion(s32[]{:T(128)} %bitcast.3, s32[]{:T(128)} %bitcast.2), kind=kLoop, calls=%fused_computation.16 | loop fusion | flops 32 | bytes 40 | tf_op jit(solution)/shard_map/lt | solution.py:332
  4.1 0.1 add_convert_fusion
  4.2 0.8 compare_select_fusion
  5.0 0.1 copy.13
  5.1 0.1 reshape.15
  5.2 0.7 pad_add_fusion.table
  5.9 55.6 %forward.1 = (f32[16,8,32,128]{3,2,1,0:T(8,128)}, bf16[64,32,128]{2,1,0:T(8,128)(2,1)}) custom-call(s32[640]{0:T(1024)} %pad_add_fusion.table, bf16[128,32,128]{2,1,0:T(8,128)(2,1)} %bitcast.13, bf16[128,32,128]{2,1,0:T(8,128)(2,1)} %bitcast.11, bf16[128,9,128,128]{3,2,1,0:T(8,128)(2,1)} %w_h.3), custom_call_target="tpu_custom_call" | custom-call | tf_op jit(solution)/shard_map/forward/pallas_call | solution.py:337
  61.4 17.0 %adjoint.1 = (f32[128,32,128]{2,1,0:T(8,128)}, f32[128,32,128]{2,1,0:T(8,128)}, f32[161,32,128]{2,1,0:T(8,128)}, bf16[160,32,128]{2,1,0:T(8,128)(2,1)}) custom-call(s32[640]{0:T(1024)} %pad_add_fusion.table, s32[1]{0:T(128)} %bitcast.4.where, f32[128,32,128]{2,1,0:T(8,128)} %bitcast.16, f32[128,32,128]{2,1,0:T(8,128)} %ctl_h.1, bf16[128,32,128]{2,1,0:T(8,128)(2,1)} %dev_h.1, ...), custom_call_target="tpu_custom_call" | custom-call | tf_op jit(solution)/shard_map/adjoint/pallas_call | solution.py:365
  78.5 13.9 %returns.1 = (bf16[128,32,128]{2,1,0:T(8,128)(2,1)}, bf16[32,32,128]{2,1,0:T(8,128)(2,1)}) custom-call(f32[161,32,128]{2,1,0:T(8,128)} %get-tuple-element.15.acc_h.acc_ref, bf16[160,32,128]{2,1,0:T(8,128)(2,1)} %get-tuple-element.16.send_ref), custom_call_target="tpu_custom_call" | custom-call | tf_op jit(solution)/shard_map/returns/pallas_call | solution.py:397
  92.4 4.2 %finish.1 = f32[128,32,128]{2,1,0:T(8,128)} custom-call(s32[640]{0:T(1024)} %pad_add_fusion.table, bf16[128,32,128]{2,1,0:T(8,128)(2,1)} %bitcast.14, f32[161,32,128]{2,1,0:T(8,128)} %get-tuple-element.15.acc_h.acc_ref, bf16[128,32,128]{2,1,0:T(8,128)(2,1)} %get-tuple-element.17.partner_ref, bf16[32,32,128]{2,1,0:T(8,128)(2,1)} %get-tuple-element.18.back_ref), custom_call_target="tpu_custom_call" | custom-call | tf_op jit(solution)/shard_map/finish/pallas_call | solution.py:417
where the time goes:
time: 97 us; the launch traced here: 96.6 us
  Pallas kernels  90.7 us (94%)
  other arithmetic  2.82 us (3%)
  local copies, waits for them, and re-layouts  2.35 us (2%)
    pallas_call x1, Pallas kernels, per_device(): pl.pallas_call(functools.partial(forward_kernel, dims), out_shape=(jax.Sh...  55.6 us
    pallas_call x1, Pallas kernels, per_device(): pl.pallas_call(functools.partial(adjoint_kernel, dims), out_shape=(jax.Sh...  17 us
    pallas_call x1, Pallas kernels, per_device(): pl.pallas_call(functools.partial(return_kernel, dims), out_shape=(jax.Sha...  13.9 us
    pallas_call x1, Pallas kernels, per_device(): pl.pallas_call(functools.partial(finish_kernel, dims), out_shape=jax.Shap...  4.21 us

commit v1 on v0

--- a/solution.py
+++ b/solution.py
@@ -38,10 +38,22 @@
     return pix, mem, core, partner, below, above
 
 
+def slot_of(names, row, s, pix, blocks, cap):
+    n = names[row, s]
+    rim = n - cap * (pix - 1) - jnp.where(n >= blocks + cap * pix, cap, 0)
+    return jnp.where(n < blocks, n, rim)
+
+
+def rim_block(outbound, counts, pix, shards, c, cap):
+    side = lax.rem(pix + (shards - 1 if c < cap else 1), shards)
+    rank = c % cap
+    return outbound[pix, side, rank], jnp.where(rank < counts[pix, side], 1.0, 0.0).astype(F32)
+
+
 def forward_kernel(
-    dims, table, alpha_h, pert_h, w_h, ens_h, other_pert_h,
+    dims, names, outbound, counts, alpha_h, pert_h, w_h, ens_h, other_pert_h,
     alpha_v, mine, theirs, pert0, pert1, wv, terms, recv, gathered, other, packed,
-    w_sem, local_sem, out_sem, pair_send, pair_recv, halo_send, halo_recv, rs_send, rs_recv, ag_send, ag_recv,
+    w_sem, local_sem, out_sem, pair_send, pair_recv, halo_send, halo_recv, rs_send, rs_recv, ag_send, ag_recv, swap_send, swap_recv,
 ):
     shards, members, blocks, neigh, cap = dims
     half, chips = blocks // 2, members // 2
@@ -64,9 +76,6 @@
         load.start()
     for step in range(chips):
         w_copy(step).start()
-    zero = jnp.zeros(mine.shape[1:], BF16)
-    mine[blocks + 2 * cap] = zero
-    theirs[blocks + 2 * cap] = zero
     peers = [(pix, 2 * lax.rem(chip + j, chips) + core) for j in range(1, chips)]
     meet([partner, below, above] + peers)
     pair = [
@@ -77,10 +86,9 @@
         ),
     ]
     loads[0].wait()
-    base = half * neigh
     for c in range(2 * cap):
-        keep = table[base + 2 * cap + c].astype(F32)
-        packed[c] = (alpha_v[table[base + c]].astype(F32) * keep).astype(BF16)
+        row, keep = rim_block(outbound, counts, pix, shards, c, cap)
+        packed[c] = (alpha_v[row].astype(F32) * keep).astype(BF16)
     halo = [
         remote(packed.at[pl.ds(0, cap)], mine.at[pl.ds(blocks + cap, cap)], halo_send.at[0], halo_recv.at[1], below),
         remote(packed.at[pl.ds(cap, cap)], mine.at[pl.ds(blocks, cap)], halo_send.at[1], halo_recv.at[0], above),
@@ -107,14 +115,14 @@
         w_copy(step).wait()
         for j in range(per):
             i = k * per + j
-            picked = [table[i * neigh + s] for s in range(neigh)]
+            picked = [slot_of(names, core * half + i, s, pix, blocks, cap) for s in range(neigh)]
             rows = jnp.concatenate(
                 [jnp.concatenate([field[n] for n in picked], axis=1) for field in (mine, theirs)], axis=0
             )
             weights = wv[i].reshape(neigh * wv.shape[2], wv.shape[3])
             local = jnp.dot(rows, weights, preferred_element_type=F32)
             ch = local.shape[0] // 2
-            terms[i] = pert0[i].astype(F32) * local[:ch] + pert1[i].astype(F32) * local[ch:]
+            terms[i] = (pert0[i].astype(F32) * local[:ch] + pert1[i].astype(F32) * local[ch:]).astype(BF16)
 
         @pl.when(step < chips - 1)
         def _():
@@ -131,29 +139,36 @@
     recv[chip] = terms[pl.ds(chip * per, per)]
     spread = 1.0 / math.sqrt(members - 1)
     for i in range(per):
-        total = recv[0, i]
+        total = recv[0, i].astype(F32)
         for k in range(1, chips):
-            total = total + recv[k, i]
-        gathered[chip, i] = total * spread
+            total = total + recv[k, i].astype(F32)
+        gathered[chip, i] = (total * spread).astype(BF16)
     sends = [
         remote(gathered.at[chip], gathered.at[chip], ag_send.at[j - 1], ag_recv.at[chip], peers[j - 1])
         for j in range(1, chips)
     ]
     for copy in sends:
         copy.start()
+
+    def swap_copy(k, j):
+        return remote(gathered.at[k], other.at[k], swap_send.at[j], swap_recv.at[k], partner)
+
+    swaps = [swap_copy(chip, 0)]
+    swaps[0].start()
     for j in range(1, chips):
         src = lax.rem(chip + j, chips)
         remote(gathered.at[src], gathered.at[src], ag_send.at[j - 1], ag_recv.at[src], partner).wait_recv()
-    swap = remote(gathered, other, pair_send.at[3], pair_recv.at[3], partner)
-    swap.start()
+        swaps.append(swap_copy(src, j))
+        swaps[j].start()
     outs = [
         pltpu.make_async_copy(gathered, ens_h.at[pl.ds(core * chips, chips)], out_sem.at[0]),
         pltpu.make_async_copy(other, ens_h.at[pl.ds((1 - core) * chips, chips)], out_sem.at[1]),
     ]
     outs[0].start()
-    swap.wait_recv()
+    for copy in swaps:
+        copy.wait_recv()
     outs[1].start()
-    for copy in halo + pair + [swap] + sends:
+    for copy in halo + pair + swaps + sends:
         copy.wait_send()
     for j in range(1, chips):
         rs_copy(lax.rem(chip + j, chips)).wait_send()
@@ -162,14 +177,14 @@
 
 
 def adjoint_kernel(
-    dims, table, where, ens_h, ctl_h, dev_h, inn_h, wgt_h, pert_h, other_pert_h, w_h, inc_h, gs_h, acc_out, send_out,
+    dims, names, ens_h, ctl_h, dev_h, inn_h, wgt_h, pert_h, other_pert_h, w_h, inc_h, gs_h, acc_out, send_out,
     ens, ctl, dev, inn, wgt, pert0, pert1, wv, inc, gs, acc0, acc1, w_sem, in_sem, out_sem,
 ):
     shards, members, blocks, neigh, cap = dims
     half = blocks // 2
     chunks = w_sem.shape[0]
     per = half // chunks
-    core = where[0]
+    pix, core = lax.axis_index("pix"), lax.rem(lax.axis_index("mem"), 2)
     spread = 1.0 / math.sqrt(members - 1)
     starts = (core * half, (1 - core) * half)
     loads = [
@@ -225,7 +240,7 @@
             )
             ch, width = focus.shape[0] // 2, wv.shape[2]
             for s in range(neigh):
-                n = table[i * neigh + s]
+                n = slot_of(names, core * half + i, s, pix, blocks, cap)
                 acc0[n] += pieces[:ch, s * width : (s + 1) * width]
                 acc1[n] += pieces[ch:, s * width : (s + 1) * width]
         return carry
@@ -252,7 +267,7 @@
         store.start()
     last = pltpu.make_async_copy(acc0, acc_out, out_sem.at[0, 2])
     last.start()
-    send_out[...] = acc1[pl.ds(0, blocks + 2 * cap)].astype(send_out.dtype)
+    send_out[...] = acc1[...].astype(send_out.dtype)
     last.wait()
     for h in range(2):
         for store in stores[h]:
@@ -292,9 +307,9 @@
         copy.wait_send()
 
 
-def finish_kernel(dims, table, alpha_ref, acc_ref, partner_ref, back_ref, out_ref):
+def finish_kernel(dims, outbound, counts, alpha_ref, acc_ref, partner_ref, back_ref, out_ref):
     shards, members, blocks, neigh, cap = dims
-    base = (blocks // 2) * neigh
+    pix = lax.axis_index("pix")
 
     def one(i, carry):
         out_ref[i] = alpha_ref[i].astype(F32) + acc_ref[i] + partner_ref[i].astype(F32)
@@ -302,7 +317,8 @@
 
     lax.fori_loop(0, blocks, one, 0, unroll=8)
     for c in range(2 * cap):
-        out_ref[table[base + c]] += back_ref[c].astype(F32) * table[base + 2 * cap + c].astype(F32)
+        row, keep = rim_block(outbound, counts, pix, shards, c, cap)
+        out_ref[row] += back_ref[c].astype(F32) * keep
 
 
 def per_device(
@@ -310,37 +326,22 @@
     send_counts,
 ):
     shards, members = lax.axis_size("pix"), lax.axis_size("mem")
-    me = lax.axis_index("pix")
-    core = lax.axis_index("mem") % 2
     alpha, pert = alpha[0], perturbations[0]
     blocks, ch, width = alpha.shape
     neigh, cap = neighbours.shape[1], outbound_blocks.shape[2]
     half, chips = blocks // 2, members // 2
-    per, ext = half // chips, blocks + 2 * cap + 1
+    per, ext = half // chips, blocks + 2 * cap
     dims = (shards, members, blocks, neigh, cap)
-
-    mine = lax.dynamic_slice_in_dim(neighbours, core * half, half, 0)
-    slot = mine - blocks
-    source = slot // cap
-    rim_slot = jnp.where(
-        source == me - 1, slot - (me - 1) * cap, jnp.where(source == me + 1, slot - me * cap, 2 * cap)
-    )
-    targets = jnp.where(mine < blocks, mine, blocks + rim_slot).reshape(half * neigh)
-    below, above = (me + shards - 1) % shards, (me + 1) % shards
-    rows = jnp.concatenate([outbound_blocks[me, below], outbound_blocks[me, above]])
-    rank = jnp.arange(cap, dtype=jnp.int32)
-    keep = jnp.concatenate([rank < send_counts[me, below], rank < send_counts[me, above]]).astype(jnp.int32)
-    table = jnp.concatenate([targets, rows, keep]).astype(jnp.int32)
 
     tile = (ch, width)
     dma = pltpu.SemaphoreType.DMA
     ens, other_pert = pl.pallas_call(
         functools.partial(forward_kernel, dims),
         out_shape=(
-            jax.ShapeDtypeStruct((members, per, *tile), F32),
+            jax.ShapeDtypeStruct((members, per, *tile), BF16),
             jax.ShapeDtypeStruct((half, *tile), BF16),
         ),
-        in_specs=[SMEM, HBM, HBM, HBM],
+        in_specs=[SMEM, SMEM, SMEM, HBM, HBM, HBM],
         out_specs=(HBM, HBM),
         scratch_shapes=[
             pltpu.VMEM((blocks, *tile), BF16),
@@ -349,17 +350,17 @@
             pltpu.VMEM((half, *tile), BF16),
             pltpu.VMEM((half, *tile), BF16),
             pltpu.VMEM((half, neigh, width, width), BF16),
-            pltpu.VMEM((half, *tile), F32),
-            pltpu.VMEM((chips, per, *tile), F32),
-            pltpu.VMEM((chips, per, *tile), F32),
-            pltpu.VMEM((chips, per, *tile), F32),
+            pltpu.VMEM((half, *tile), BF16),
+            pltpu.VMEM((chips, per, *tile), BF16),
+            pltpu.VMEM((chips, per, *tile), BF16),
+            pltpu.VMEM((chips, per, *tile), BF16),
             pltpu.VMEM((2 * cap, *tile), BF16),
-            dma((chips,)), dma((3,)), dma((3,)), dma((4,)), dma((4,)), dma((2,)), dma((2,)),
-            dma((chips,)), dma((chips,)), dma((chips,)), dma((chips,)),
+            dma((chips,)), dma((3,)), dma((3,)), dma((3,)), dma((3,)), dma((2,)), dma((2,)),
+            dma((chips,)), dma((chips,)), dma((chips,)), dma((chips,)), dma((chips,)), dma((chips,)),
         ],
         compiler_params=pltpu.CompilerParams(collective_id=0, has_side_effects=True, vmem_limit_bytes=LIMIT),
         name="forward",
-    )(table, alpha, pert, loc_weights)
+    )(neighbours, outbound_blocks, send_counts, alpha, pert, loc_weights)
 
     chunks = max(half // 8, 1)
     increment, grad_static, acc, sending = pl.pallas_call(
@@ -368,12 +369,12 @@
             jax.ShapeDtypeStruct((blocks, *tile), F32),
             jax.ShapeDtypeStruct((blocks, *tile), F32),
             jax.ShapeDtypeStruct((ext, *tile), F32),
-            jax.ShapeDtypeStruct((ext - 1, *tile), BF16),
+            jax.ShapeDtypeStruct((ext, *tile), BF16),
         ),
-        in_specs=[SMEM, SMEM] + [HBM] * 8,
+        in_specs=[SMEM] + [HBM] * 8,
         out_specs=(HBM, HBM, HBM, VMEM),
         scratch_shapes=[
-            pltpu.VMEM((2, half, *tile), F32),
+            pltpu.VMEM((2, half, *tile), BF16),
             pltpu.VMEM((2, half, *tile), F32),
             pltpu.VMEM((2, half, *tile), BF16),
             pltpu.VMEM((2, half, *tile), F32),
@@ -390,7 +391,7 @@
         compiler_params=pltpu.CompilerParams(vmem_limit_bytes=LIMIT),
         name="adjoint",
     )(
-        table, core.reshape(1), ens.reshape(blocks, *tile), static_ctl, static_sd, innovation, obs_weight, pert,
+        neighbours, ens.reshape(blocks, *tile), static_ctl, static_sd, innovation, obs_weight, pert,
         other_pert, loc_weights,
     )
 
@@ -417,11 +418,11 @@
     grad_alpha = pl.pallas_call(
         functools.partial(finish_kernel, dims),
         out_shape=jax.ShapeDtypeStruct((blocks, *tile), F32),
-        in_specs=[SMEM, VMEM, VMEM, VMEM, VMEM],
+        in_specs=[SMEM, SMEM, VMEM, VMEM, VMEM, VMEM],
         out_specs=VMEM,
         compiler_params=pltpu.CompilerParams(vmem_limit_bytes=LIMIT),
         name="finish",
-    )(table, alpha, acc, from_partner, came_back)
+    )(outbound_blocks, send_counts, alpha, acc, from_partner, came_back)
     return increment, grad_static, grad_alpha[None]
 
 

time: 97 us -> 79.1 us (0.82)
  Pallas kernels: 90.7 us -> 76.6 us
  other arithmetic: 2.82 us -> 0 us
    pallas_call x1, Pallas kernels: 55.6 us -> 42 us  [per_device(): pl.pallas_call(functools.partial(forward_kernel, dims), out_shape=(jax.Sh...]
    unnamed x0 -> x1, local copies, waits for them, and re-layouts: none -> 1.42 us
    dynamic_slice x1 -> x0, local copies, waits for them, and re-layouts: 1.35 us -> none  [per_device(): send_counts[me, below]]
    lt x1 -> x0, other arithmetic: 1.3 us -> none  [per_device(): rank < send_counts[me, above]]
    pallas_call x1, Pallas kernels: 13.9 us -> 12.7 us  [per_device(): pl.pallas_call(functools.partial(return_kernel, dims), out_shape=(jax.Sha...]
where the time goes in v1:
time: 79.1 us; the launch traced here: 78.7 us
  Pallas kernels  76.6 us (97%)
  local copies, waits for them, and re-layouts  1.42 us (2%)
    pallas_call x1, Pallas kernels, per_device(): pl.pallas_call(functools.partial(forward_kernel, dims), out_shape=(jax.Sh...  42 us
    pallas_call x1, Pallas kernels, per_device(): pl.pallas_call(functools.partial(adjoint_kernel, dims), out_shape=(jax.Sh...  17.7 us
    pallas_call x1, Pallas kernels, per_device(): pl.pallas_call(functools.partial(return_kernel, dims), out_shape=(jax.Sha...  12.7 us
    pallas_call x1, Pallas kernels, per_device(): pl.pallas_call(functools.partial(finish_kernel, dims), out_shape=jax.Shap...  4.2 us

profile of v1, /device:TPU:1, one launch (start us, length us, event | category | flops | bytes accessed | tf_op | source)
XLA Modules:
  0.0 78.7 jit_solution(10213649944581040754)
XLA Ops:
  0.6 1.4 %copy.14.names = s32[128,9]{1,0:T(8,128)} copy(s32[128,9]{0,1:T(8,128)} %param.17) | data formatting | bytes 9216 | tf_op args[7]
  2.0 42.0 %forward.1 = (bf16[16,8,32,128]{3,2,1,0:T(8,128)(2,1)}, bf16[64,32,128]{2,1,0:T(8,128)(2,1)}) custom-call(s32[128,9]{1,0:T(8,128)} %copy.14.names, s32[8,8,16]{2,1,0:T(8,128)} %outbound.3, s32[8,8]{1,0:T(8,128)} %counts.3, bf16[128,32,128]{2,1,0:T(8,128)(2,1)} %bitcast.6, bf16[128,32,128]{2,1,0:T(8,128)(2,1)} %bitcast.4, bf16[128,9,128,128]{3,2,1,0:T(8,128)(2,1)} %w_h.3), custom_call_target="tpu_custom_call" | custom-call | tf_op jit(solution)/shard_map/forward/pallas_call | solution.py:338
  44.0 17.7 %adjoint.1 = (f32[128,32,128]{2,1,0:T(8,128)}, f32[128,32,128]{2,1,0:T(8,128)}, f32[160,32,128]{2,1,0:T(8,128)}, bf16[160,32,128]{2,1,0:T(8,128)(2,1)}) custom-call(s32[128,9]{1,0:T(8,128)} %copy.14.names, bf16[128,32,128]{2,1,0:T(8,128)(2,1)} %bitcast.9, f32[128,32,128]{2,1,0:T(8,128)} %ctl_h.1, bf16[128,32,128]{2,1,0:T(8,128)(2,1)} %dev_h.1, ...), custom_call_target="tpu_custom_call" | custom-call | tf_op jit(solution)/shard_map/adjoint/pallas_call | solution.py:366
  61.8 12.7 %returns.1 = (bf16[128,32,128]{2,1,0:T(8,128)(2,1)}, bf16[32,32,128]{2,1,0:T(8,128)(2,1)}) custom-call(f32[160,32,128]{2,1,0:T(8,128)} %get-tuple-element.15.acc_h.acc_ref, bf16[160,32,128]{2,1,0:T(8,128)(2,1)} %get-tuple-element.16.send_ref), custom_call_target="tpu_custom_call" | custom-call | tf_op jit(solution)/shard_map/returns/pallas_call | solution.py:398
  74.5 4.2 %finish.1 = f32[128,32,128]{2,1,0:T(8,128)} custom-call(s32[8,8,16]{2,1,0:T(8,128)} %outbound.3, s32[8,8]{1,0:T(8,128)} %counts.3, bf16[128,32,128]{2,1,0:T(8,128)(2,1)} %bitcast.7, f32[160,32,128]{2,1,0:T(8,128)} %get-tuple-element.15.acc_h.acc_ref, bf16[128,32,128]{2,1,0:T(8,128)(2,1)} %get-tuple-element.17.partner_ref, ...), custom_call_target="tpu_custom_call" | custom-call | tf_op jit(solution)/shard_map/finish/pallas_call | solution.py:418
